TPU v7x, 32 devices: a whole 2x2x4 slice. The times are simulated.
32 devices in a mesh: az: 8 (over z, x), rx: 4 (over y, core).
Axes of the slice: x: 2, y: 2, z: 4, core: 2. Of those that a mesh axis runs over, the one named last changes fastest.
Arguments:
- adjoint: float32 [5, 8, 128, 512], P(None, 'az', None, 'rx'), may hold values from -6 to 6
- density: float32 [8, 128, 512], P('az', None, 'rx'), may hold values from 0.6 to 1.4
- velocity: float32 [3, 8, 128, 512], P(None, 'az', None, 'rx'), may hold values from -0.9 to 0.9
- pressure: float32 [8, 128, 512], P('az', None, 'rx'), may hold values from 0.5 to 0.9
- fwh_cell: int32 [8, 4, 256], P('az', 'rx'), may hold values from 0 to 16383
- fwh_bin: int32 [8, 4, 256], P('az', 'rx'), may hold values from 0 to 255
- fwh_weight: float32 [8, 4, 256], P('az', 'rx'), may hold values from -6 to 6
- fwh_count: int32 [8, 4], P('az', 'rx'), may hold values from 1 to 256, as said below
Outputs:
- section: float32 [5, 8, 128, 512], P(None, 'az', None, 'rx')
- signal: float32 [256], P(('az', 'rx'))
Inputs may be any that keep to these rules, and one draw needn't show every extreme that they name: `fwh_count`: slots at or after a device's count are unused; some device has all 256 slots live.
All inputs are finite; a program needn't handle non-finite values.
Results may differ from a plain program's by a relative error of at most 0.00017.
Values sent between devices are 32-bit elements; how exact they have to be, the bound alone decides.
No kernel may reach another device: no remote copies, remote signals or barrier semaphores. Data moves between devices by JAX's collectives and lax.ppermute only.
A program may use at most 64 MiB of HBM per device.

v0:
```python
import math
import jax
import jax.numpy as jnp
from jax import lax
from jax.sharding import PartitionSpec as P

BIN_DEV = 8
ALPHA_FILTER = 0.495
COEF_ZERO = 11.0 / 16.0 + 5.0 * ALPHA_FILTER / 8.0
COEF_ONE = 15.0 / 32.0 + 17.0 * ALPHA_FILTER / 16.0
COEF_TWO = -3.0 / 16.0 + 3.0 * ALPHA_FILTER / 8.0
COEF_THREE = 1.0 / 32.0 - ALPHA_FILTER / 16.0
ALPHA_DERIV = 1.0 / 3.0
NEAR_COEF = 14.0 / 9.0
FAR_COEF = 1.0 / 9.0
AXIAL_STEP = 0.02
RADIAL_STEP = 0.02
INNER_RADIUS = 0.3
SECTION_STEP = 0.004
GAMMA_GAS = 1.4


def padded_2(shard, sides, width):
    for axis, dim in sides:
        size, length = (lax.axis_size(axis), shard.shape[dim])
        up = [(i, (i + 1) % size) for i in range(size - 1)]
        down = [(j, i) for i, j in up]
        last = lax.slice_in_dim(shard, length - width, length, axis=dim)
        leading = lax.slice_in_dim(shard, 0, width, axis=dim)
        before = lax.ppermute(last, axis, up)
        after = lax.ppermute(leading, axis, down)
        shard = jnp.concatenate([before, shard, after], axis=dim)
    return shard


def mode_gains(count):
    angle = jnp.arange(count, dtype=jnp.int32).astype(jnp.float32) * (2.0 * math.pi / count)
    cosine = jnp.cos(angle)
    filter_gain = (
        COEF_ZERO
        + COEF_ONE * cosine
        + COEF_TWO * jnp.cos(2.0 * angle)
        + COEF_THREE * jnp.cos(3.0 * angle)
    ) / (1.0 + 2.0 * ALPHA_FILTER * cosine)
    spacing = 2.0 * math.pi / count
    deriv_gain = (
        filter_gain
        * (NEAR_COEF * jnp.sin(angle) + 0.5 * FAR_COEF * jnp.sin(2.0 * angle))
        / (spacing * (1.0 + 2.0 * ALPHA_DERIV * cosine))
    )
    return (filter_gain, deriv_gain)


def kernel_values(offsets, count, filter_gain, deriv_gain):
    modes = jnp.arange(count, dtype=jnp.int32)
    phase = jnp.mod(offsets[..., None] * modes, count).astype(jnp.float32) * (2.0 * math.pi / count)
    smooth = jnp.sum(filter_gain * jnp.cos(phase), axis=-1) / count
    slope = -jnp.sum(deriv_gain * jnp.sin(phase), axis=-1) / count
    return (smooth, slope)


def central(padded, axis, width, step):

    def piece_at(start):
        return lax.slice_in_dim(padded, start, start + width, axis=axis)

    return (
        45.0 * (piece_at(4) - piece_at(2))
        - 9.0 * (piece_at(5) - piece_at(1))
        + (piece_at(6) - piece_at(0))
    ) / (60.0 * step)


def adjoint_flux(grad_axial, grad_radial, grad_theta, density, velocity, pressure):
    axial_vel, radial_vel, swirl_vel = (velocity[0], velocity[1], velocity[2])
    stiff = GAMMA_GAS * pressure
    inverse = 1.0 / density
    mass_term = axial_vel * grad_axial[0] + radial_vel * grad_radial[0] + swirl_vel * grad_theta[0]
    axial_term = (
        density * grad_axial[0]
        + axial_vel * grad_axial[1]
        + stiff * grad_axial[4]
        + radial_vel * grad_radial[1]
        + swirl_vel * grad_theta[1]
    )
    radial_term = (
        axial_vel * grad_axial[2]
        + density * grad_radial[0]
        + radial_vel * grad_radial[2]
        + stiff * grad_radial[4]
        + swirl_vel * grad_theta[2]
    )
    swirl_term = (
        axial_vel * grad_axial[3]
        + radial_vel * grad_radial[3]
        + density * grad_theta[0]
        + swirl_vel * grad_theta[3]
        + stiff * grad_theta[4]
    )
    energy_term = (
        inverse * grad_axial[1]
        + axial_vel * grad_axial[4]
        + inverse * grad_radial[2]
        + radial_vel * grad_radial[4]
        + inverse * grad_theta[3]
        + swirl_vel * grad_theta[4]
    )
    return jnp.stack([mass_term, axial_term, radial_term, swirl_term, energy_term])


def local(adjoint, density, velocity, pressure, fwh_cell, fwh_bin, fwh_weight, fwh_count):
    fields, local_theta, radial_cells, axial_cells = adjoint.shape
    count = local_theta * lax.axis_size("az")
    filter_gain, deriv_gain = mode_gains(count)
    piece = lax.all_gather(adjoint, "az", axis=1, tiled=True)
    width = piece.shape[1]
    targets = lax.axis_index("az") * local_theta + jnp.arange(local_theta, dtype=jnp.int32)
    sources = jnp.arange(width, dtype=jnp.int32)
    offsets = jnp.mod(targets[:, None] - sources[None, :], count)
    smooth, slope = kernel_values(offsets, count, filter_gain, deriv_gain)
    filtered = jnp.einsum("ij,cjrx->cirx", smooth, piece, precision=lax.Precision.HIGHEST)
    dtheta = jnp.einsum("ij,cjrx->cirx", slope, piece, precision=lax.Precision.HIGHEST)
    pad_axial = padded_2(filtered, (("rx", 3),), 3)
    daxial = central(pad_axial, 3, axial_cells, AXIAL_STEP)
    pad_radial = jnp.pad(filtered, ((0, 0), (0, 0), (3, 3), (0, 0)))
    dradial = central(pad_radial, 2, radial_cells, RADIAL_STEP)
    radius = (
        INNER_RADIUS
        + (jnp.arange(radial_cells, dtype=jnp.int32).astype(jnp.float32) + 0.5) * RADIAL_STEP
    ).reshape(radial_cells, 1)
    flux = adjoint_flux(daxial, dradial, dtheta / radius, density, velocity, pressure)
    section = filtered + SECTION_STEP * flux
    slot_cells = fwh_cell[0, 0]
    slot_bins = fwh_bin[0, 0]
    slot_weights = fwh_weight[0, 0]
    live = jnp.arange(slot_cells.shape[0], dtype=jnp.int32) < fwh_count[0, 0]
    picked = jnp.take(section.reshape(fields, -1), slot_cells, axis=1)
    values = jnp.where(live, slot_weights * (picked[4] + picked[1]), 0.0)
    totals = jax.ops.segment_sum(
        values, slot_bins, num_segments=BIN_DEV * lax.axis_size("az") * lax.axis_size("rx")
    )
    signal = lax.psum_scatter(totals, ("az", "rx"), scatter_dimension=0, tiled=True)
    return (section, signal)


def solution(mesh):
    placed = (
        P(None, "az", None, "rx"),
        P("az", None, "rx"),
        P(None, "az", None, "rx"),
        P("az", None, "rx"),
        P("az", "rx", None),
        P("az", "rx", None),
        P("az", "rx", None),
        P("az", "rx"),
    )
    return jax.shard_map(
        local,
        mesh=mesh,
        in_specs=placed,
        out_specs=(P(None, "az", None, "rx"), P(("az", "rx"))),
        check_vma=False,
    )
```

profile of v0, /device:TPU:0, one launch (start us, length us, event | category | flops | bytes accessed | tf_op | source)
XLA Modules:
  0.0 143.3 jit_solution(1472916147521559716)
XLA Ops:
  7.2 0.0 all-gather.2.cloned.1.call-start
  7.2 0.7 all-gather.2.cloned.1.call-update
  8.6 0.1 multiply_divide_fusion
  8.6 0.7 compare_select_fusion
  9.3 0.2 multiply_reduce_fusion
  9.6 0.7 compare_and_fusion
  10.3 57.3 %all-gather.2.cloned.1.call-done = f32[5,8,128,128]{3,2,1,0:T(8,128)} async-done(((f32[5,1,128,128]{3,2,1,0:T(8,128)}), f32[5,8,128,128]{3,2,1,0:T(8,128)}) %all-gather.2.cloned.1.call-update) | async-done | bytes 2621456 | tf_op jit(solution)/shard_map/all_gather | solution.py:115
  67.6 0.0 copy-start
  67.6 5.4 %fusion.2 = f32[1,5,128,128]{3,0,2,1:T(1,128)S(1)} fusion(f32[5,8,128,128]{3,2,1,0:T(8,128)} %all-gather.2.cloned.1.call-done, f32[8]{0:T(128)S(1)} %get-tuple-element.3), kind=kOutput, calls=%fused_computation.4 | convolution fusion | flops 7864328 | bytes 2949152 | tf_op jit(solution)/shard_map/ij,cjrx->cirx/dot_general | solution.py:121
  73.0 0.2 fusion.62
  73.2 1.3 collective-permute-start
  74.5 3.1 %collective-permute-start.1 = (f32[5,1,128,3]{3,2,1,0:T(8,128)S(1)}, f32[5,1,128,3]{3,2,1,0:T(8,128)S(1)}, u32[]{:S(2)}, u32[]{:S(2)}) collective-permute-start(f32[5,1,128,3]{3,2,1,0:T(8,128)S(1)} %get-tuple-element.7), channel_id=1, source_target_pairs={{0,1},{1,2},{2,3},{4,5},{5,6},{6,7},{8,9},{9,10},{10,11},{12,13},{... | collective-permute-start | bytes 23048 | tf_op jit(solution)/shard_map/ppermute | solution.py:30
  77.5 0.0 copy-done
  77.5 0.0 copy-start.1
  77.5 0.0 copy-start.3
  77.6 0.0 copy-start.4
  77.6 3.6 %fusion = f32[1,5,128,128]{3,0,2,1:T(1,128)S(1)} fusion(f32[5,8,128,128]{3,2,1,0:T(8,128)S(1)} %copy-done, f32[8]{0:T(128)S(1)} %get-tuple-element.2), kind=kOutput, calls=%fused_computation.2 | convolution fusion | flops 7864336 | bytes 2949152 | tf_op jit(solution)/shard_map/ij,cjrx->cirx/dot_general | solution.py:122
  81.1 0.1 broadcast_divide_fusion
  81.2 0.0 collective-permute-done
  81.2 0.0 collective-permute-done.1
  81.3 1.1 fusion.9
  82.4 0.0 copy-done.1
  82.5 0.0 copy-done.3
  82.5 0.0 copy-done.4
  82.7 0.0 copy-start.2
  82.7 0.0 copy-start.5
  82.7 4.7 %copy.13 = f32[5,128,128]{0,2,1:T(8,128)} copy(f32[5,128,128]{2,1,0:T(8,128)S(1)} %multiply_add_fusion) | data formatting | bytes 655360 | tf_op jit(solution)/shard_map/add | solution.py:132
  87.4 0.0 copy-done.2
  87.4 4.1 %gather_fusion = f32[256,5]{1,0:T(8,128)S(1)} fusion(f32[5,16384]{0,1:T(8,128)} %bitcast.150, s32[1024]{0:T(1024)S(1)} %pad_clamp_fusion), kind=kCustom, calls=%fused_computation | custom fusion | bytes 11264 | tf_op jit(solution)/shard_map/jit(_take)/gather | solution.py:137
  91.5 0.1 select_bitcast_fusion
  91.6 0.2 fusion.16
  91.9 0.0 copy-done.5
  91.9 2.5 %scatter_custom_fusion = f32[256]{0:T(256)S(1)} fusion(s32[256]{0:T(256)} %bitcast.159, f32[256]{0:T(256)S(1)} %compare_select_fusion.4, f32[]{:T(128)} %constant.83.clone.1), kind=kCustom, calls=%fused_computation.103 | custom fusion | flops 256 | bytes 1536 | tf_op jit(solution)/shard_map/scatter-add | solution.py:139
  94.3 41.5 %all-reduce.1 = f32[256]{0:T(256)S(1)} all-reduce(f32[256]{0:T(256)S(1)} %scatter_custom_fusion), channel_id=2, replica_groups=mesh['az'=8,'rx'=4] {'az','rx'}, use_global_device_ids=true, to_apply=%region_3.4.clone | all-reduce | flops 256 | bytes 2048
  135.9 0.6 dynamic-slice
  (10 shorter events, 0.3 us)
Async XLA Ops:
  7.2 60.4 %all-gather.2.cloned.1.call-start = ((), (), s32[]{:S(2)}) async-start(), calls=%async_computation | async-start | bytes 2949120 | tf_op jit(solution)/shard_map/all_gather | solution.py:115
  67.6 10.0 %copy-start = (f32[5,8,128,128]{3,2,1,0:T(8,128)S(1)}, f32[5,8,128,128]{3,2,1,0:T(8,128)}, u32[]{:S(2)}) copy-start(f32[5,8,128,128]{3,2,1,0:T(8,128)} %all-gather.2.cloned.1.call-done) | copy-start | bytes 7864324
  73.2 8.1 %collective-permute-start = (f32[5,1,128,3]{3,2,1,0:T(8,128)S(1)}, f32[5,1,128,3]{3,2,1,0:T(8,128)S(1)}, u32[]{:S(2)}, u32[]{:S(2)}) collective-permute-start(f32[5,1,128,3]{3,2,1,0:T(8,128)S(1)} %get-tuple-element.6), channel_id=1, source_target_pairs={{1,0},{2,1},{3,2},{5,4},{6,5},{7,6},{9,8},{10,9},{11,10},{13,12},{... | collective-permute-start | bytes 23048 | tf_op jit(solution)/shard_map/ppermute | solution.py:31
  74.5 6.8 %collective-permute-start.1 = (f32[5,1,128,3]{3,2,1,0:T(8,128)S(1)}, f32[5,1,128,3]{3,2,1,0:T(8,128)S(1)}, u32[]{:S(2)}, u32[]{:S(2)}) collective-permute-start(f32[5,1,128,3]{3,2,1,0:T(8,128)S(1)} %get-tuple-element.7), channel_id=1, source_target_pairs={{0,1},{1,2},{2,3},{4,5},{5,6},{6,7},{8,9},{9,10},{10,11},{12,13},{... | collective-permute-start | bytes 23048 | tf_op jit(solution)/shard_map/ppermute | solution.py:30
  77.5 4.9 %copy-start.1 = (f32[3,1,128,128]{3,2,1,0:T(8,128)S(1)}, f32[3,1,128,128]{3,2,1,0:T(8,128)}, u32[]{:S(2)}) copy-start(f32[3,1,128,128]{3,2,1,0:T(8,128)} %param.10) | copy-start | bytes 589828
  77.5 4.9 %copy-start.3 = (f32[1,128,128]{2,1,0:T(8,128)S(1)}, f32[1,128,128]{2,1,0:T(8,128)}, u32[]{:S(2)}) copy-start(f32[1,128,128]{2,1,0:T(8,128)} %param.9) | copy-start | bytes 196612
  77.6 4.9 %copy-start.4 = (f32[1,128,128]{2,1,0:T(8,128)S(1)}, f32[1,128,128]{2,1,0:T(8,128)}, u32[]{:S(2)}) copy-start(f32[1,128,128]{2,1,0:T(8,128)} %param.11) | copy-start | bytes 196612
  82.7 4.7 %copy-start.2 = (f32[5,128,128]{2,1,0:T(8,128)}, f32[5,128,128]{2,1,0:T(8,128)S(1)}, u32[]{:S(2)}) copy-start(f32[5,128,128]{2,1,0:T(8,128)S(1)} %multiply_add_fusion) | copy-start | bytes 983044
  82.7 9.2 %copy-start.5 = (f32[1,1,256]{2,1,0:T(1,128)S(1)}, f32[1,1,256]{2,1,0:T(1,128)}, u32[]{:S(2)}) copy-start(f32[1,1,256]{2,1,0:T(1,128)} %param.14) | copy-start | bytes 3076
Sparse Core Ops, SparseCore 0:
  10.2 57.3 all-gather.1
where the time goes:
time: 144 us; the launch traced here: 143 us
  waiting for transfers between devices  58 us (40%)
  blocking collectives  41.5 us (29%)
  between operations  14.9 us (10%)
  local copies, waits for them, and re-layouts  9.59 us (7%)
  matrix products  8.98 us (6%)
  other arithmetic  5.92 us (4%)
  starting transfers between devices  4.38 us (3%)
    all_gather x1, waiting for transfers between devices, local(): piece = lax.all_gather(adjoint, 'az', axis=1, tiled=True)  57.3 us
    unnamed x1, blocking collectives  41.5 us
    dot_general x1, matrix products, local(): jnp.einsum('ij,cjrx->cirx', smooth, piece, precision=lax.Precision.HIGHEST)  5.43 us
    add x1, local copies, waits for them, and re-layouts, local(): section = filtered + SECTION_STEP * flux  4.71 us
    gather x1, local copies, waits for them, and re-layouts, local(): picked = jnp.take(section.reshape(fields, -1), slot_cells, axis=1)  4.1 us
    dot_general x1, matrix products, local(): jnp.einsum('ij,cjrx->cirx', slope, piece, precision=lax.Precision.HIGHEST)  3.56 us
    ppermute x1, starting transfers between devices, padded_2(): before = lax.ppermute(last, axis, up)  3.05 us
  transfers between devices with their start and end apart: 3, of which 1 were waited for; matrix products, arithmetic and copies ran while one was open for 4% of the time, Pallas kernels for 0%

commit v1 on v0

--- a/solution.py
+++ b/solution.py
@@ -18,6 +18,19 @@
 INNER_RADIUS = 0.3
 SECTION_STEP = 0.004
 GAMMA_GAS = 1.4
+
+
+def ring_gather(array, axis, dim):
+    ways = lax.axis_size(axis)
+    up = [(d, (d + 1) % ways) for d in range(ways)]
+    down = [(d, (d - 1) % ways) for d in range(ways)]
+    earlier, later = ([array], [array])
+    for _ in range(ways // 2):
+        earlier.append(lax.ppermute(earlier[-1], axis, up))
+    for _ in range((ways - 1) // 2):
+        later.append(lax.ppermute(later[-1], axis, down))
+    line = jnp.concatenate([*earlier[::-1], *later[1:]], axis=dim)
+    return jnp.roll(line, (lax.axis_index(axis) - ways // 2) * array.shape[dim], axis=dim)
 
 
 def padded_2(shard, sides, width):
@@ -112,7 +125,7 @@
     fields, local_theta, radial_cells, axial_cells = adjoint.shape
     count = local_theta * lax.axis_size("az")
     filter_gain, deriv_gain = mode_gains(count)
-    piece = lax.all_gather(adjoint, "az", axis=1, tiled=True)
+    piece = ring_gather(adjoint, "az", 1)
     width = piece.shape[1]
     targets = lax.axis_index("az") * local_theta + jnp.arange(local_theta, dtype=jnp.int32)
     sources = jnp.arange(width, dtype=jnp.int32)

time: 144 us -> 133 us (0.924)
  starting transfers between devices: 4.38 us -> 22.2 us
  waiting for transfers between devices: 58 us -> 41.6 us
  between operations: 14.9 us -> 1.63 us
  local copies, waits for them, and re-layouts: 9.59 us -> 11.2 us
    all_gather x1 -> x0, waiting for transfers between devices: 57.3 us -> none  [local(): piece = lax.all_gather(adjoint, 'az', axis=1, tiled=True)]
    ppermute x0 -> x7, waiting for transfers between devices: none -> 38.6 us  [the longest x4 37.1 us: ring_gather(): earlier.append(lax.ppermute(earlier[-1], axis, up))]
    ppermute x0 -> x7, starting transfers between devices: none -> 18.8 us  [the longest x3 11 us: ring_gather(): later.append(lax.ppermute(later[-1], axis, down))]
    ppermute x1, waiting for transfers between devices: 0.01 us -> 3.03 us  [padded_2(): after = lax.ppermute(leading, axis, down)]
    dot_general x1, matrix products: 5.43 us -> 3.85 us  [local(): jnp.einsum('ij,cjrx->cirx', smooth, piece, precision=lax.Precision.HIGHEST)]
  transfers between devices with their start and end apart: 3 -> 9, of which waited for: 1 -> 6; matrix products, arithmetic and copies ran while one was open for 4% -> 2% of each run, Pallas kernels for 0% -> 0%
where the time goes in v1:
time: 133 us; the launch traced here: 132 us
  blocking collectives  42 us (32%)
  waiting for transfers between devices  41.6 us (31%)
  starting transfers between devices  22.2 us (17%)
  local copies, waits for them, and re-layouts  11.2 us (8%)
  matrix products  7.7 us (6%)
  other arithmetic  5.91 us (4%)
  between operations  1.63 us (1%)
    unnamed x1, blocking collectives  42 us
    ppermute x4, waiting for transfers between devices, ring_gather(): earlier.append(lax.ppermute(earlier[-1], axis, up))  37.1 us
    ppermute x3, starting transfers between devices, ring_gather(): later.append(lax.ppermute(later[-1], axis, down))  11 us
    ppermute x4, starting transfers between devices, ring_gather(): earlier.append(lax.ppermute(earlier[-1], axis, up))  7.85 us
    add x1, local copies, waits for them, and re-layouts, local(): section = filtered + SECTION_STEP * flux  4.69 us
    gather x1, local copies, waits for them, and re-layouts, local(): picked = jnp.take(section.reshape(fields, -1), slot_cells, axis=1)  4.1 us
    dot_general x1, matrix products, local(): jnp.einsum('ij,cjrx->cirx', smooth, piece, precision=lax.Precision.HIGHEST)  3.85 us
    dot_general x1, matrix products, local(): jnp.einsum('ij,cjrx->cirx', slope, piece, precision=lax.Precision.HIGHEST)  3.85 us
  transfers between devices with their start and end apart: 9, of which 6 were waited for; matrix products, arithmetic and copies ran while one was open for 2% of the time, Pallas kernels for 0%

profile of v1, /device:TPU:0, one launch (start us, length us, event | category | flops | bytes accessed | tf_op | source)
XLA Modules:
  0.0 132.3 jit_solution(7361754063797236016)
XLA Ops:
  0.6 0.0 copy-start.2
  0.6 3.0 %collective-permute-start = (f32[5,1,128,128]{3,2,1,0:T(8,128)}, f32[5,1,128,128]{3,2,1,0:T(8,128)S(1)}, u32[]{:S(2)}, u32[]{:S(2)}) collective-permute-start(f32[5,1,128,128]{3,2,1,0:T(8,128)} %param.8), channel_id=1, source_target_pairs={{0,4},{4,8},{8,12},{12,16},{16,20},{20,24},{24,28},{28,0},{1,5},{5... | collective-permute-start | bytes 983048 | tf_op jit(solution)/shard_map/ppermute | solution.py:29
  3.6 3.1 %collective-permute-start.4 = (f32[5,1,128,128]{3,2,1,0:T(8,128)}, f32[5,1,128,128]{3,2,1,0:T(8,128)S(1)}, u32[]{:S(2)}, u32[]{:S(2)}) collective-permute-start(f32[5,1,128,128]{3,2,1,0:T(8,128)} %param.8), channel_id=1, source_target_pairs={{0,28},{4,0},{8,4},{12,8},{16,12},{20,16},{24,20},{28,24},{1,29},{... | collective-permute-start | bytes 983048 | tf_op jit(solution)/shard_map/ppermute | solution.py:31
  7.4 10.5 %collective-permute-done = f32[5,1,128,128]{3,2,1,0:T(8,128)S(1)} collective-permute-done((f32[5,1,128,128]{3,2,1,0:T(8,128)}, f32[5,1,128,128]{3,2,1,0:T(8,128)S(1)}, u32[]{:S(2)}, u32[]{:S(2)}) %collective-permute-start) | collective-permute-done | bytes 327712 | tf_op jit(solution)/shard_map/ppermute | solution.py:29
  17.9 2.4 %collective-permute-start.1 = (f32[5,1,128,128]{3,2,1,0:T(8,128)S(1)}, f32[5,1,128,128]{3,2,1,0:T(8,128)S(1)}, u32[]{:S(2)}, u32[]{:S(2)}) collective-permute-start(f32[5,1,128,128]{3,2,1,0:T(8,128)S(1)} %collective-permute-done), channel_id=1, source_target_pairs={{0,4},{4,8},{8,12},{12,16},{16,20},{20,24},{24,28},{28,0},{1,5},{5... | collective-permute-start | bytes 983048 | tf_op jit(solution)/shard_map/ppermute | solution.py:29
  20.3 0.1 multiply_divide_fusion
  20.4 0.7 compare_select_fusion
  21.1 9.1 %collective-permute-done.1 = f32[5,1,128,128]{3,2,1,0:T(8,128)S(1)} collective-permute-done((f32[5,1,128,128]{3,2,1,0:T(8,128)S(1)}, f32[5,1,128,128]{3,2,1,0:T(8,128)S(1)}, u32[]{:S(2)}, u32[]{:S(2)}) %collective-permute-start.1) | collective-permute-done | bytes 327712 | tf_op jit(solution)/shard_map/ppermute | solution.py:29
  30.2 0.0 collective-permute-start.2
  30.2 0.2 multiply_reduce_fusion
  30.4 0.0 collective-permute-done.4
  30.5 4.8 %collective-permute-start.5 = (f32[5,1,128,128]{3,2,1,0:T(8,128)S(1)}, f32[5,1,128,128]{3,2,1,0:T(8,128)S(1)}, u32[]{:S(2)}, u32[]{:S(2)}) collective-permute-start(f32[5,1,128,128]{3,2,1,0:T(8,128)S(1)} %collective-permute-done.4), channel_id=1, source_target_pairs={{0,28},{4,0},{8,4},{12,8},{16,12},{20,16},{24,20},{28,24},{1,29},{... | collective-permute-start | bytes 983048 | tf_op jit(solution)/shard_map/ppermute | solution.py:31
  35.2 7.7 %collective-permute-done.2 = f32[5,1,128,128]{3,2,1,0:T(8,128)S(1)} collective-permute-done((f32[5,1,128,128]{3,2,1,0:T(8,128)S(1)}, f32[5,1,128,128]{3,2,1,0:T(8,128)S(1)}, u32[]{:S(2)}, u32[]{:S(2)}) %collective-permute-start.2) | collective-permute-done | bytes 327712 | tf_op jit(solution)/shard_map/ppermute | solution.py:29
  43.0 2.5 %collective-permute-start.3 = (f32[5,1,128,128]{3,2,1,0:T(8,128)S(1)}, f32[5,1,128,128]{3,2,1,0:T(8,128)S(1)}, u32[]{:S(2)}, u32[]{:S(2)}) collective-permute-start(f32[5,1,128,128]{3,2,1,0:T(8,128)S(1)} %collective-permute-done.2), channel_id=1, source_target_pairs={{0,4},{4,8},{8,12},{12,16},{16,20},{20,24},{24,28},{28,0},{1,5},{5... | collective-permute-start | bytes 983048 | tf_op jit(solution)/shard_map/ppermute | solution.py:29
  45.4 0.7 compare_and_fusion
  46.1 0.0 collective-permute-done.5
  46.1 3.1 %collective-permute-start.6 = (f32[5,1,128,128]{3,2,1,0:T(8,128)S(1)}, f32[5,1,128,128]{3,2,1,0:T(8,128)S(1)}, u32[]{:S(2)}, u32[]{:S(2)}) collective-permute-start(f32[5,1,128,128]{3,2,1,0:T(8,128)S(1)} %collective-permute-done.5), channel_id=1, source_target_pairs={{0,28},{4,0},{8,4},{12,8},{16,12},{20,16},{24,20},{28,24},{1,29},{... | collective-permute-start | bytes 983048 | tf_op jit(solution)/shard_map/ppermute | solution.py:31
  49.2 9.7 %collective-permute-done.3 = f32[5,1,128,128]{3,2,1,0:T(8,128)S(1)} collective-permute-done((f32[5,1,128,128]{3,2,1,0:T(8,128)S(1)}, f32[5,1,128,128]{3,2,1,0:T(8,128)S(1)}, u32[]{:S(2)}, u32[]{:S(2)}) %collective-permute-start.3) | collective-permute-done | bytes 327712 | tf_op jit(solution)/shard_map/ppermute | solution.py:29
  59.0 1.0 constant_dynamic-update-slice_fusion.11
  60.1 1.5 %collective-permute-done.6 = f32[5,1,128,128]{3,2,1,0:T(8,128)S(1)} collective-permute-done((f32[5,1,128,128]{3,2,1,0:T(8,128)S(1)}, f32[5,1,128,128]{3,2,1,0:T(8,128)S(1)}, u32[]{:S(2)}, u32[]{:S(2)}) %collective-permute-start.6) | collective-permute-done | bytes 327712 | tf_op jit(solution)/shard_map/ppermute | solution.py:31
  61.8 0.0 copy-done.2
  61.9 0.3 constant_dynamic-slice_fusion
  62.2 0.0 copy-start
  62.2 0.0 copy-start.3
  62.2 0.0 copy-start.4
  62.2 3.9 %fusion.2 = f32[1,5,128,128]{3,0,2,1:T(1,128)S(1)} fusion(f32[5,8,128,128]{3,2,1,0:T(8,128)S(1)} %constant_dynamic-slice_fusion, f32[8]{0:T(128)S(1)} %get-tuple-element.3), kind=kOutput, calls=%fused_computation.4 | convolution fusion | flops 7864328 | bytes 2949152 | tf_op jit(solution)/shard_map/ij,cjrx->cirx/dot_general | solution.py:134
  66.1 3.9 %fusion = f32[1,5,128,128]{3,0,2,1:T(1,128)S(1)} fusion(f32[5,8,128,128]{3,2,1,0:T(8,128)S(1)} %constant_dynamic-slice_fusion, f32[8]{0:T(128)S(1)} %get-tuple-element.2), kind=kOutput, calls=%fused_computation.2 | convolution fusion | flops 7864336 | bytes 2949152 | tf_op jit(solution)/shard_map/ij,cjrx->cirx/dot_general | solution.py:135
  70.0 0.2 fusion.62
  70.1 1.9 %collective-permute-start.8 = (f32[5,1,128,3]{3,2,1,0:T(8,128)S(1)}, f32[5,1,128,3]{3,2,1,0:T(8,128)S(1)}, u32[]{:S(2)}, u32[]{:S(2)}) collective-permute-start(f32[5,1,128,3]{3,2,1,0:T(8,128)S(1)} %get-tuple-element.7), channel_id=1, source_target_pairs={{0,1},{1,2},{2,3},{4,5},{5,6},{6,7},{8,9},{9,10},{10,11},{12,13},{... | collective-permute-start | bytes 23048 | tf_op jit(solution)/shard_map/ppermute | solution.py:43
  72.1 1.5 %collective-permute-start.7 = (f32[5,1,128,3]{3,2,1,0:T(8,128)S(1)}, f32[5,1,128,3]{3,2,1,0:T(8,128)S(1)}, u32[]{:S(2)}, u32[]{:S(2)}) collective-permute-start(f32[5,1,128,3]{3,2,1,0:T(8,128)S(1)} %get-tuple-element.6), channel_id=1, source_target_pairs={{1,0},{2,1},{3,2},{5,4},{6,5},{7,6},{9,8},{10,9},{11,10},{13,12},{... | collective-permute-start | bytes 23048 | tf_op jit(solution)/shard_map/ppermute | solution.py:44
  73.5 0.1 broadcast_divide_fusion
  73.6 0.0 collective-permute-done.8
  73.7 3.0 %collective-permute-done.7 = f32[5,1,128,3]{3,2,1,0:T(8,128)S(1)} collective-permute-done((f32[5,1,128,3]{3,2,1,0:T(8,128)S(1)}, f32[5,1,128,3]{3,2,1,0:T(8,128)S(1)}, u32[]{:S(2)}, u32[]{:S(2)}) %collective-permute-start.7) | collective-permute-done | bytes 7712 | tf_op jit(solution)/shard_map/ppermute | solution.py:44
  76.7 1.1 fusion.9
  77.8 0.0 copy-done
  77.9 0.0 copy-done.3
  77.9 0.0 copy-done.4
  78.1 0.0 copy-start.5
  78.1 0.0 copy-start.1
  78.2 4.7 %copy.13 = f32[5,128,128]{0,2,1:T(8,128)} copy(f32[5,128,128]{2,1,0:T(8,128)S(1)} %multiply_add_fusion) | data formatting | bytes 655360 | tf_op jit(solution)/shard_map/add | solution.py:145
  82.8 4.1 %gather_fusion = f32[256,5]{1,0:T(8,128)S(1)} fusion(f32[5,16384]{0,1:T(8,128)} %bitcast.148, s32[1024]{0:T(1024)S(1)} %pad_clamp_fusion), kind=kCustom, calls=%fused_computation | custom fusion | bytes 11264 | tf_op jit(solution)/shard_map/jit(_take)/gather | solution.py:150
  86.9 0.1 select_bitcast_fusion
  87.1 0.2 fusion.16
  87.3 0.0 copy-done.5
  87.3 2.5 %scatter_custom_fusion = f32[256]{0:T(256)S(1)} fusion(s32[256]{0:T(256)} %bitcast.157, f32[256]{0:T(256)S(1)} %compare_select_fusion.4, f32[]{:T(128)} %constant.102.clone.1), kind=kCustom, calls=%fused_computation.119 | custom fusion | flops 256 | bytes 1536 | tf_op jit(solution)/shard_map/scatter-add | solution.py:152
  89.7 42.0 %all-reduce.1 = f32[256]{0:T(256)S(1)} all-reduce(f32[256]{0:T(256)S(1)} %scatter_custom_fusion), channel_id=2, replica_groups=mesh['az'=8,'rx'=4] {'az','rx'}, use_global_device_ids=true, to_apply=%region_3.4.clone | all-reduce | flops 256 | bytes 2048
  131.7 0.6 dynamic-slice
  132.3 0.0 copy-done.1
  (25 shorter events, 0.6 us)
Async XLA Ops:
  0.6 61.1 %copy-start.2 = (f32[5,1,128,128]{3,2,1,0:T(8,128)S(1)}, f32[5,1,128,128]{3,2,1,0:T(8,128)}, u32[]{:S(2)}) copy-start(f32[5,1,128,128]{3,2,1,0:T(8,128)} %param.8) | copy-start | bytes 983044
  0.6 17.3 %collective-permute-start = (f32[5,1,128,128]{3,2,1,0:T(8,128)}, f32[5,1,128,128]{3,2,1,0:T(8,128)S(1)}, u32[]{:S(2)}, u32[]{:S(2)}) collective-permute-start(f32[5,1,128,128]{3,2,1,0:T(8,128)} %param.8), channel_id=1, source_target_pairs={{0,4},{4,8},{8,12},{12,16},{16,20},{20,24},{24,28},{28,0},{1,5},{5... | collective-permute-start | bytes 983048 | tf_op jit(solution)/shard_map/ppermute | solution.py:29
  3.6 26.8 %collective-permute-start.4 = (f32[5,1,128,128]{3,2,1,0:T(8,128)}, f32[5,1,128,128]{3,2,1,0:T(8,128)S(1)}, u32[]{:S(2)}, u32[]{:S(2)}) collective-permute-start(f32[5,1,128,128]{3,2,1,0:T(8,128)} %param.8), channel_id=1, source_target_pairs={{0,28},{4,0},{8,4},{12,8},{16,12},{20,16},{24,20},{28,24},{1,29},{... | collective-permute-start | bytes 983048 | tf_op jit(solution)/shard_map/ppermute | solution.py:31
  17.9 12.2 %collective-permute-start.1 = (f32[5,1,128,128]{3,2,1,0:T(8,128)S(1)}, f32[5,1,128,128]{3,2,1,0:T(8,128)S(1)}, u32[]{:S(2)}, u32[]{:S(2)}) collective-permute-start(f32[5,1,128,128]{3,2,1,0:T(8,128)S(1)} %collective-permute-done), channel_id=1, source_target_pairs={{0,4},{4,8},{8,12},{12,16},{16,20},{20,24},{24,28},{28,0},{1,5},{5... | collective-permute-start | bytes 983048 | tf_op jit(solution)/shard_map/ppermute | solution.py:29
  30.2 12.8 %collective-permute-start.2 = (f32[5,1,128,128]{3,2,1,0:T(8,128)S(1)}, f32[5,1,128,128]{3,2,1,0:T(8,128)S(1)}, u32[]{:S(2)}, u32[]{:S(2)}) collective-permute-start(f32[5,1,128,128]{3,2,1,0:T(8,128)S(1)} %collective-permute-done.1), channel_id=1, source_target_pairs={{0,4},{4,8},{8,12},{12,16},{16,20},{20,24},{24,28},{28,0},{1,5},{5... | collective-permute-start | bytes 983048 | tf_op jit(solution)/shard_map/ppermute | solution.py:29
  30.5 15.7 %collective-permute-start.5 = (f32[5,1,128,128]{3,2,1,0:T(8,128)S(1)}, f32[5,1,128,128]{3,2,1,0:T(8,128)S(1)}, u32[]{:S(2)}, u32[]{:S(2)}) collective-permute-start(f32[5,1,128,128]{3,2,1,0:T(8,128)S(1)} %collective-permute-done.4), channel_id=1, source_target_pairs={{0,28},{4,0},{8,4},{12,8},{16,12},{20,16},{24,20},{28,24},{1,29},{... | collective-permute-start | bytes 983048 | tf_op jit(solution)/shard_map/ppermute | solution.py:31
  43.0 16.0 %collective-permute-start.3 = (f32[5,1,128,128]{3,2,1,0:T(8,128)S(1)}, f32[5,1,128,128]{3,2,1,0:T(8,128)S(1)}, u32[]{:S(2)}, u32[]{:S(2)}) collective-permute-start(f32[5,1,128,128]{3,2,1,0:T(8,128)S(1)} %collective-permute-done.2), channel_id=1, source_target_pairs={{0,4},{4,8},{8,12},{12,16},{16,20},{20,24},{24,28},{28,0},{1,5},{5... | collective-permute-start | bytes 983048 | tf_op jit(solution)/shard_map/ppermute | solution.py:29
  46.1 15.5 %collective-permute-start.6 = (f32[5,1,128,128]{3,2,1,0:T(8,128)S(1)}, f32[5,1,128,128]{3,2,1,0:T(8,128)S(1)}, u32[]{:S(2)}, u32[]{:S(2)}) collective-permute-start(f32[5,1,128,128]{3,2,1,0:T(8,128)S(1)} %collective-permute-done.5), channel_id=1, source_target_pairs={{0,28},{4,0},{8,4},{12,8},{16,12},{20,16},{24,20},{28,24},{1,29},{... | collective-permute-start | bytes 983048 | tf_op jit(solution)/shard_map/ppermute | solution.py:31
  62.2 15.6 %copy-start = (f32[3,1,128,128]{3,2,1,0:T(8,128)S(1)}, f32[3,1,128,128]{3,2,1,0:T(8,128)}, u32[]{:S(2)}) copy-start(f32[3,1,128,128]{3,2,1,0:T(8,128)} %param.10) | copy-start | bytes 589828
  62.2 15.7 %copy-start.3 = (f32[1,128,128]{2,1,0:T(8,128)S(1)}, f32[1,128,128]{2,1,0:T(8,128)}, u32[]{:S(2)}) copy-start(f32[1,128,128]{2,1,0:T(8,128)} %param.9) | copy-start | bytes 196612
  62.2 15.7 %copy-start.4 = (f32[1,128,128]{2,1,0:T(8,128)S(1)}, f32[1,128,128]{2,1,0:T(8,128)}, u32[]{:S(2)}) copy-start(f32[1,128,128]{2,1,0:T(8,128)} %param.11) | copy-start | bytes 196612
  70.1 3.5 %collective-permute-start.8 = (f32[5,1,128,3]{3,2,1,0:T(8,128)S(1)}, f32[5,1,128,3]{3,2,1,0:T(8,128)S(1)}, u32[]{:S(2)}, u32[]{:S(2)}) collective-permute-start(f32[5,1,128,3]{3,2,1,0:T(8,128)S(1)} %get-tuple-element.7), channel_id=1, source_target_pairs={{0,1},{1,2},{2,3},{4,5},{5,6},{6,7},{8,9},{9,10},{10,11},{12,13},{... | collective-permute-start | bytes 23048 | tf_op jit(solution)/shard_map/ppermute | solution.py:43
  72.1 4.6 %collective-permute-start.7 = (f32[5,1,128,3]{3,2,1,0:T(8,128)S(1)}, f32[5,1,128,3]{3,2,1,0:T(8,128)S(1)}, u32[]{:S(2)}, u32[]{:S(2)}) collective-permute-start(f32[5,1,128,3]{3,2,1,0:T(8,128)S(1)} %get-tuple-element.6), channel_id=1, source_target_pairs={{1,0},{2,1},{3,2},{5,4},{6,5},{7,6},{9,8},{10,9},{11,10},{13,12},{... | collective-permute-start | bytes 23048 | tf_op jit(solution)/shard_map/ppermute | solution.py:44
  78.1 9.2 %copy-start.5 = (f32[1,1,256]{2,1,0:T(1,128)S(1)}, f32[1,1,256]{2,1,0:T(1,128)}, u32[]{:S(2)}) copy-start(f32[1,1,256]{2,1,0:T(1,128)} %param.14) | copy-start | bytes 3076
  78.1 54.2 %copy-start.1 = (f32[5,128,128]{2,1,0:T(8,128)}, f32[5,128,128]{2,1,0:T(8,128)S(1)}, u32[]{:S(2)}) copy-start(f32[5,128,128]{2,1,0:T(8,128)S(1)} %multiply_add_fusion) | copy-start | bytes 983044
